TPU v7x, 32 devices: a whole 2x2x4 slice. The times are simulated.
32 devices in a mesh: dp: 8 (over z, x), tensor: 4 (over y, core).
Axes of the slice: x: 2, y: 2, z: 4, core: 2. Of those that a mesh axis runs over, the one named last changes fastest.
Arguments:
- images_in: bfloat16 [32, 544, 768], P(('dp', 'tensor')), may hold values from -6 to 6
- crop_lengths: int32 [32, 6], P('dp'), may hold values from 1 to 197, 544 in all within a row
- route_index: int32 [32, 272], P('dp'), may hold values from 0 to 543, as said below
- router_weight: bfloat16 [768], replicated, may hold values from -0.21875 to 0.21875
- norm_gain: bfloat16 [2, 2, 768], replicated, may hold values from 0.5 to 1.5
- norm_shift: bfloat16 [2, 2, 768], replicated, may hold values from -1.75 to 1.75
- qkv_weight: bfloat16 [2, 3, 768, 768], P(None, None, None, 'tensor'), may hold values from -0.21875 to 0.21875
- qv_bias: bfloat16 [2, 2, 768], P(None, None, 'tensor'), may hold values from -3 to 3
- out_weight: bfloat16 [2, 768, 768], P(None, 'tensor'), may hold values from -0.75 to 0.75
- out_bias: bfloat16 [2, 768], replicated, may hold values from -1.75 to 1.75
- fc1_weight: bfloat16 [2, 768, 3072], P(None, None, 'tensor'), may hold values from -0.21875 to 0.21875
- fc1_bias: bfloat16 [2, 3072], P(None, 'tensor'), may hold values from -3 to 3
- fc2_weight: bfloat16 [2, 3072, 768], P(None, 'tensor'), may hold values from -0.109375 to 0.109375
- fc2_bias: bfloat16 [2, 768], replicated, may hold values from -1.75 to 1.75
- out_cotangent: bfloat16 [32, 544, 768], P(('dp', 'tensor')), may hold values from -6 to 6
Outputs:
- images_out: bfloat16 [32, 544, 768], P(('dp', 'tensor'))
- input_grad: float32 [32, 544, 768], P(('dp', 'tensor'))
- router_grad: float32 [768], replicated
- gain_grad: float32 [2, 2, 768], replicated
- shift_grad: float32 [2, 2, 768], replicated
- qkv_grad: float32 [2, 3, 768, 768], P(None, None, None, 'tensor')
- qv_bias_grad: float32 [2, 2, 768], P(None, None, 'tensor')
- out_weight_grad: float32 [2, 768, 768], P(None, 'tensor')
- out_bias_grad: float32 [2, 768], replicated
- fc1_grad: float32 [2, 768, 3072], P(None, None, 'tensor')
- fc1_bias_grad: float32 [2, 3072], P(None, 'tensor')
- fc2_grad: float32 [2, 3072, 768], P(None, 'tensor')
- fc2_bias_grad: float32 [2, 768], replicated
Inputs may be any that keep to these rules, and one draw needn't show every extreme that they name: `route_index`: within each image the 272 positions are distinct and ascending.
All inputs are finite; a program needn't handle non-finite values.
Results may differ from a plain program's by a relative error of at most 0.02.
Values may be sent and summed in bfloat16 or wider, within the bound.
A program may use at most 256 MiB of HBM per device.

v0:
```python
import functools

import jax
import jax.numpy as jnp
from jax import lax
from jax.experimental import pallas as pl
from jax.experimental.pallas import tpu as pltpu
from jax.sharding import PartitionSpec as P

HEAD_DIM = 64
HID_TILE = 256

norm_eps = 1e-06
mask_fill = -1e30
half_root = 0.7071067811865476
inv_root_tau = 0.3989422804014327

F32 = jnp.float32
BF16 = jnp.bfloat16
NN = (((1,), (0,)), ((), ()))
NT = (((1,), (1,)), ((), ()))
TN = (((0,), (0,)), ((), ()))


def mm(a, b, dims):
    return lax.dot_general(a, b, dims, preferred_element_type=F32)


def norm_parts(rows):
    centred = rows - jnp.mean(rows, axis=-1, keepdims=True)
    inv_std = lax.rsqrt(jnp.mean(centred * centred, axis=-1, keepdims=True) + norm_eps)
    return centred * inv_std, inv_std


def gelu_parts(preact):
    decay = jnp.exp(-0.5 * preact * preact)
    t = 1.0 / (1.0 + 0.3275911 * half_root * jnp.abs(preact))
    series = 1.421413741 + t * (-1.453152027 + t * 1.061405429)
    series = t * (0.254829592 + t * (-0.284496736 + t * series))
    tail = 0.5 * series * decay
    return jnp.where(preact >= 0.0, 1.0 - tail, tail), decay


def pick_rows(ones, rows):
    high = rows.astype(BF16)
    rest = rows - high.astype(F32)
    middle = rest.astype(BF16)
    low = (rest - middle.astype(F32)).astype(BF16)
    return mm(ones, high, NN) + (mm(ones, middle, NN) + mm(ones, low, NN))


any_spec = pl.BlockSpec(memory_space=pl.ANY)


MESH = pl.DeviceIdType.MESH


class Place:
    def __init__(self, n_data):
        self.data, self.tensor = lax.axis_index("dp"), lax.axis_index("tensor")
        self.bits = [1 << b for b in range(n_data.bit_length() - 1)]
        self.sides = [lax.rem(self.data // bit, 2) for bit in self.bits]

    def by_tensor(self, bit):
        own = lax.rem(self.tensor // bit, 2)
        return (self.data, self.tensor + bit * (1 - 2 * own))

    def by_data(self, number):
        bit = self.bits[number]
        return (self.data + bit * (1 - 2 * self.sides[number]), self.tensor)


def greet(partners):
    barrier = pltpu.get_barrier_semaphore()
    for partner in partners:
        pl.semaphore_signal(barrier, inc=1, device_id=partner, device_id_type=MESH)
    pl.semaphore_wait(barrier, len(partners))


def remote(src, dst, send_sem, recv_sem, device):
    return pltpu.make_async_remote_copy(
        src_ref=src,
        dst_ref=dst,
        send_sem=send_sem,
        recv_sem=recv_sem,
        device_id=device,
        device_id_type=MESH,
    )


KINDS = ("y", "z", "x", "core_y", "core_z", "core_x")


class Gather:
    def __init__(self, place, own, got, sends, recvs, near_sems, small, small_sends, small_recvs):
        self.own, self.got, self.sends, self.recvs = own, got, sends, recvs
        self.near_sems, self.units = near_sems, len(own)
        self.core, self.across = place.by_tensor(1), place.by_tensor(2)
        self.side_x, self.side_z = place.by_data(0), place.by_data(1)
        x, self.z = place.sides[0], place.sides[1]
        self.half = got.shape[2] // 6
        self.thirds = {
            "y": x * (1 - self.z) + 2 * self.z,
            "z": 2 * (1 - self.z) + x * self.z,
            "x": 1 - x,
            "x_out": x,
        }
        self.count = 2 * self.units
        self.little = [
            remote(small.at[0], small.at[1], small_sends.at[0], small_recvs.at[0], self.core),
            remote(small.at[0], small.at[2], small_sends.at[1], small_recvs.at[1], self.across),
            remote(small.at[2], small.at[3], small_sends.at[2], small_recvs.at[2], self.core),
        ]

    def copy(self, v, kind):
        u, number = v // 2, KINDS.index(kind)
        sems = (self.sends.at[v, number], self.recvs.at[v, number])
        third = self.thirds[{"y": "y", "z": "y", "x": "x_out"}.get(kind, kind[-1])]
        at = pl.multiple_of((2 * third + v % 2) * self.half, self.half)
        rows = pl.ds(at, self.half)
        here = self.got.at[u, 1, rows]
        if kind == "y":
            source = self.own[u].at[rows] if isinstance(v, int) else here
            return remote(source, here, *sems, self.across)
        if kind in ("z", "x"):
            return remote(here, here, *sems, self.side_z if kind == "z" else self.side_x)
        return remote(here, self.got.at[u, 2, rows], *sems, self.core)

    def near_copy(self, u):
        sems = (self.near_sems.at[0, u], self.near_sems.at[1, u])
        return remote(self.own[u], self.got.at[u, 0], *sems, self.core)

    def start(self, shards):
        self.little[0].start()
        self.little[1].start()
        shards[0].wait()
        self.copy(0, "y").start()
        self.copy(1, "y").start()
        self.near_copy(0).start()
        for v in range(2, 6):
            self.copy(v, "y").start()
        shards[1].wait()
        for v in range(6, self.count):
            self.copy(v, "y").start()
        for u in range(1, self.units):
            self.near_copy(u).start()

    def turn(self, k):
        @pl.when(k < self.count)
        def _():
            self.copy(k, "y").wait_recv()
            self.copy(k, "z").start()

            @pl.when(self.z == 0)
            def _():
                self.copy(k, "x").start()

            self.copy(k, "core_y").start()

        @pl.when(jnp.logical_and(k >= 1, k < self.count + 1))
        def _():
            self.copy(k - 1, "z").wait_recv()

            @pl.when(self.z == 1)
            def _():
                self.copy(k - 1, "x").start()

            self.copy(k - 1, "core_z").start()

        @pl.when(k >= 2)
        def _():
            self.copy(k - 2, "x").wait_recv()
            self.copy(k - 2, "core_x").start()

    def turns(self, first, last):
        def run(k, carry):
            self.turn(k)
            return carry

        lax.fori_loop(first, last, run, 0)

    def small_turn(self):
        self.little[1].wait_recv()
        self.little[2].start()
        self.little[0].wait_recv()
        self.little[2].wait_recv()

    def near(self, u):
        self.near_copy(u).wait_recv()

    def far(self, u):
        def run(v, carry):
            for kind in ("core_y", "core_z", "core_x"):
                self.copy(v, kind).wait_recv()
            return carry

        lax.fori_loop(2 * u, 2 * u + 2, run, 0)

    def finish(self):
        for item in self.little:
            item.wait_send()
        for u in range(self.units):
            self.near_copy(u).wait_send()

        def run(v, carry):
            for kind in KINDS:
                self.copy(v, kind).wait_send()
            return carry

        lax.fori_loop(0, self.count, run, 0)


def split_in_two(region, side):
    row, n_rows, lane, n_lanes = region
    if n_rows >= 32:
        half = n_rows // 2
        keep = (pl.multiple_of(row + side * half, half), half, lane, n_lanes)
        give = (pl.multiple_of(row + (1 - side) * half, half), half, lane, n_lanes)
    else:
        half = n_lanes // 2
        keep = (row, n_rows, pl.multiple_of(lane + side * half, half), half)
        give = (row, n_rows, pl.multiple_of(lane + (1 - side) * half, half), half)
    return keep, give


def piece_shapes(n_bits, rows, lanes):
    shapes = []
    for _ in range(n_bits):
        rows, lanes = (rows // 2, lanes) if rows >= 32 else (rows, lanes // 2)
        shapes.append((rows, lanes))
    return shapes


SLOTS = 6


class Sums:
    def __init__(self, place, units, outs, buffers):
        self.count, self.units, self.outs = 18, units, outs
        self.own, self.far, self.got_own, self.got_far, self.got_y, self.total = buffers[:6]
        self.got_bits, self.sends, self.recvs, self.loads, self.stores = buffers[6:11]
        self.turned = buffers[11]
        self.rows, self.lanes = self.own.shape[1:]
        self.n_bits = len(place.bits)
        self.core, self.across = place.by_tensor(1), place.by_tensor(2)
        self.partners = [place.by_data(i) for i in range(self.n_bits)]
        self.keeps, self.gives = [], []
        region = (0, self.rows, 0, self.lanes)
        for i in range(self.n_bits):
            region, give = split_in_two(region, place.sides[i])
            self.keeps.append(region)
            self.gives.append(give)
        halves = [functools.partial(self.halve, i) for i in range(self.n_bits)]
        doubles = [functools.partial(self.double, i) for i in reversed(range(self.n_bits))]
        self.stages = [self.load_far, self.sum_far, self.load_own, self.sum_own, None]
        self.stages += halves + doubles[:-1] + [None] + doubles[-1:] + [self.retire]

    def add(self, dst, a, b):
        dst[...] = (a[...].astype(F32) + b[...].astype(F32)).astype(BF16)

    def view(self, ref, slot, region):
        row, n_rows, lane, n_lanes = region
        return ref.at[slot, pl.ds(row, n_rows), pl.ds(lane, n_lanes)]

    def entry(self, c):
        layer, place = c // 9, lax.rem(c, 9)
        attn = place // 6
        unit = 3 * layer + 2 * attn + (1 - attn) * (1 - lax.rem(place, 2))
        part = attn * (place - 6) + (1 - attn) * (place // 2)
        return unit, part, (1 - attn) * lax.rem(place, 2)

    def pair(self, number, c):
        unit, part, _ = self.entry(c)
        rows = pl.ds(pl.multiple_of(part * self.rows, self.rows), self.rows)
        slot = lax.rem(c, SLOTS)
        got, mine = ((self.got_far, self.far), (self.got_own, self.own))[number]
        give, keep = ((3, 2), (1, 0))[number]
        return (
            remote(
                self.units.at[unit, give, rows], got.at[slot], self.sends.at[number, c],
                self.recvs.at[number, c], self.core,
            ),
            pltpu.make_async_copy(self.units.at[unit, keep, rows], mine.at[slot], self.loads.at[number, c]),
        )

    def y_copy(self, c):
        slot = lax.rem(c, SLOTS)
        return remote(
            self.far.at[slot], self.got_y.at[slot], self.sends.at[2, c], self.recvs.at[2, c],
            self.across,
        )

    def halve_copy(self, i, c):
        return remote(
            self.view(self.own, lax.rem(c, SLOTS), self.gives[i]),
            self.got_bits[i].at[lax.rem(c, SLOTS)],
            self.sends.at[3 + i, c],
            self.recvs.at[3 + i, c],
            self.partners[i],
        )

    def double_copy(self, i, c):
        number = 3 + self.n_bits + i
        piece = self.view(self.total, lax.rem(c, SLOTS), self.keeps[i])
        return remote(
            piece, piece, self.sends.at[number, c], self.recvs.at[number, c], self.partners[i]
        )

    def store_copy(self, c, turned):
        unit, part, _ = self.entry(c)
        at = pl.ds(pl.multiple_of(part * self.rows, self.rows), self.rows)
        if turned:
            return pltpu.make_async_copy(
                self.turned.at[lax.rem(c, 2)], self.outs.at[unit, :, at], self.stores.at[c]
            )
        return pltpu.make_async_copy(
            self.total.at[lax.rem(c, SLOTS)], self.outs.at[unit, at], self.stores.at[c]
        )

    def both(self, c, act):
        turned = self.entry(c)[2]

        @pl.when(turned == 1)
        def _():
            act(True)

        @pl.when(turned == 0)
        def _():
            act(False)

    def store(self, c):
        def act(turned):
            if turned:
                self.turned[lax.rem(c, 2)] = jnp.transpose(self.total[lax.rem(c, SLOTS)])
            self.store_copy(c, turned).start()

        self.both(c, act)

    def load(self, number, c):
        for item in self.pair(number, c):
            item.start()

    def load_far(self, c):
        self.load(0, c)

    def load_own(self, c):
        self.load(1, c)

    def sum_far(self, c):
        for item in self.pair(0, c):
            item.wait()
        far = self.far.at[lax.rem(c, SLOTS)]
        self.add(far, far, self.got_far.at[lax.rem(c, SLOTS)])
        self.y_copy(c).start()

    def sum_own(self, c):
        for item in self.pair(1, c):
            item.wait()
        slot = lax.rem(c, SLOTS)
        self.y_copy(c).wait()
        own = self.own[slot].astype(F32) + self.got_own[slot].astype(F32)
        self.own[slot] = (own + self.got_y[slot].astype(F32)).astype(BF16)
        self.halve_copy(0, c).start()

    def halve(self, i, c):
        self.halve_copy(i, c).wait()
        slot = lax.rem(c, SLOTS)
        kept = self.view(self.own, slot, self.keeps[i])
        got = self.got_bits[i].at[lax.rem(c, SLOTS)]
        if i + 1 < self.n_bits:
            self.add(kept, kept, got)
            self.halve_copy(i + 1, c).start()
        else:
            self.add(self.view(self.total, slot, self.keeps[i]), kept, got)
            self.double_copy(i, c).start()

    def double(self, i, c):
        self.double_copy(i, c).wait()
        if i > 0:
            self.double_copy(i - 1, c).start()
        else:
            self.store(c)

    def retire(self, c):
        self.both(c, lambda turned: self.store_copy(c, turned).wait())

    def turn(self, t):
        last = len(self.stages) - 1
        for number in [last] + list(range(last)):
            if self.stages[number] is not None:
                c = t - number

                @pl.when(jnp.logical_and(c >= 0, c < self.count))
                def _():
                    self.stages[number](c)


class Butterfly:
    def __init__(self, place, stages, got, sends, recvs):
        self.stages, self.got, self.sends, self.recvs = stages, got, sends, recvs
        self.n_bits = len(place.bits)
        self.ways = [place.by_data(i) for i in range(self.n_bits)]
        self.ways += [place.by_tensor(1), place.by_tensor(2)]
        self.head = stages.shape[1] - 8 * 4

    def copy(self, i):
        return remote(
            self.stages.at[i], self.got.at[i], self.sends.at[i], self.recvs.at[i], self.ways[i]
        )

    def turn(self, i):
        if i > 0:
            self.copy(i - 1).wait()
            stages, got, head = self.stages, self.got, self.head
            if i - 1 < self.n_bits:
                stages[i] = stages[i - 1] + got[i - 1]
            else:
                bit = 1 << (i - 1 - self.n_bits)
                stages[i, 0:head] = stages[i - 1, 0:head] + got[i - 1, 0:head]
                for block in range(4):
                    at = slice(head + 8 * block, head + 8 * block + 8)
                    there = slice(head + 8 * (block ^ bit), head + 8 * (block ^ bit) + 8)
                    stages[i, at] = stages[i - 1, at] + got[i - 1, there]
        if i < len(self.ways):
            self.copy(i).start()


def loop(count, turn):
    def step(i, carry):
        turn(i)
        return carry

    lax.fori_loop(0, count, step, 0)


def norm_back(g_normed, u, gain):
    xhat, inv_std = norm_parts(u)
    scaled = g_normed * gain
    inner = jnp.mean(scaled, axis=-1, keepdims=True) + xhat * jnp.mean(
        scaled * xhat, axis=-1, keepdims=True
    )
    return (
        inv_std * (scaled - inner),
        jnp.sum(g_normed * xhat, axis=0, keepdims=True),
        jnp.sum(g_normed, axis=0, keepdims=True),
    )


class Names:
    def __init__(self, names, refs):
        for name, ref in zip(names, refs, strict=True):
            setattr(self, name, ref)


def fetch(block, own, got, then):
    @pl.when(block == 0)
    def _():
        then(own)

    @pl.when(block != 0)
    def _():
        then(got.at[jnp.maximum(block - 1, 0)])


def attention_forward_phase(r, layer, rows_ref, crops, acc, before):
    length = crops[0].shape[0]
    own = r.attn.at[layer]
    got = r.got.at[3 * layer]
    qkv, ho = (r.qkv0, r.ho0) if layer == 0 else (r.qkv1, r.ho1)
    width = ho.shape[2]
    tile = length // 2 if length > 320 else length
    scale = HEAD_DIM**-0.5

    def begin(s):
        slot = lax.rem(s, 2)
        fetch(
            s, own, got,
            lambda src: pltpu.make_async_copy(src, r.wa.at[slot], r.w_sems.at[slot, 0]).start(),
        )

    def step(s):
        slot = lax.rem(s, 2)
        before(s)

        @pl.when(slot == 0)
        def _():
            begin(s)
            begin(s + 1)

        pltpu.make_async_copy(own, r.wa.at[slot], r.w_sems.at[slot, 0]).wait()
        projected = mm(rows_ref[0:length], r.wa[slot, 0 : 3 * width], NT)
        at = 2 * width * layer
        q = (projected[:, 0:width] + r.small[s, :, at : at + width]).astype(BF16)
        qkv[s, :, 0:width] = q * BF16(scale)
        qkv[s, :, width : 2 * width] = projected[:, width : 2 * width].astype(BF16)
        v = projected[:, 2 * width : 3 * width] + r.small[s, :, at + width : at + 2 * width]
        qkv[s, :, 2 * width : 3 * width] = v.astype(BF16)
        for head in range(width // HEAD_DIM):
            first = head * HEAD_DIM
            keys = qkv[s, :, width + first : width + first + HEAD_DIM]
            vals = qkv[s, :, 2 * width + first : 2 * width + first + HEAD_DIM]
            for part in range(length // tile):
                here = slice(part * tile, (part + 1) * tile)
                scores = mm(qkv[s, here, first : first + HEAD_DIM], keys, NT)
                scores = jnp.where(crops[0][here] == crops[1][...], scores, mask_fill)
                top = jnp.max(scores, axis=-1, keepdims=True)
                weight = jnp.exp(scores - top)
                total = jnp.sum(weight, axis=-1, keepdims=True)
                head_out = mm(weight.astype(BF16), vals, NN) / total
                ho[s, here, first : first + HEAD_DIM] = head_out.astype(BF16)
        acc[0:length] += mm(ho[s], r.wa[slot, 3 * width : 4 * width], NN)

    loop(4, step)


def hidden_bias(r, layer, block, tile):
    hidden = r.fc1.shape[2]
    at = r.small.shape[2] - (2 - layer) * hidden + tile * HID_TILE
    return r.small[block, :, pl.ds(pl.multiple_of(at, HID_TILE), HID_TILE)]


def ffn_forward_phase(r, layer, length, rows_ref, acc, before):
    own1, own2 = r.fc1.at[layer], r.fc2.at[layer]
    got1, got2 = r.got.at[3 * layer + 1], r.got.at[3 * layer + 2]
    tiles = own1.shape[1] // HID_TILE
    steps = 4 * tiles

    def begin(s):
        block, slot = s // tiles, lax.rem(s, 2)
        cols = pl.ds(pl.multiple_of(lax.rem(s, tiles) * HID_TILE, HID_TILE), HID_TILE)
        fetch(
            block, own1, got1,
            lambda src: pltpu.make_async_copy(
                src.at[:, cols], r.w1.at[slot], r.w_sems.at[slot, 0]
            ).start(),
        )
        fetch(
            block, own2, got2,
            lambda src: pltpu.make_async_copy(
                src.at[cols], r.w2.at[slot], r.w_sems.at[slot, 1]
            ).start(),
        )

    begin(0)

    def step(s):
        slot = lax.rem(s, 2)
        before(s)

        @pl.when(s == steps // 2)
        def _():
            begin(s)

        @pl.when(jnp.logical_and(s + 1 != steps // 2, s + 1 < steps))
        def _():
            begin(s + 1)

        pltpu.make_async_copy(
            own1.at[:, pl.ds(0, HID_TILE)], r.w1.at[slot], r.w_sems.at[slot, 0]
        ).wait()
        pltpu.make_async_copy(
            own2.at[pl.ds(0, HID_TILE)], r.w2.at[slot], r.w_sems.at[slot, 1]
        ).wait()
        preact = mm(rows_ref[0:length], r.w1[slot], NN)
        preact = preact + hidden_bias(r, layer, s // tiles, lax.rem(s, tiles))
        half, _ = gelu_parts(preact)
        acc[0:length] += mm((preact * half).astype(BF16), r.w2[slot], NN)

    loop(steps, step)


def ffn_phase(r, layer, length, low, rows_ref, acc_out, acc_back, targets, b1_row, after):
    own1, own2 = r.fc1.at[layer], r.fc2.at[layer]
    got1, got2 = r.got.at[3 * layer + 1], r.got.at[3 * layer + 2]
    tiles = own1.shape[1] // HID_TILE
    steps = 4 * tiles
    head = r.little.shape[1] - 32

    def where_is(s):
        return s // 4, 3 - lax.rem(s, 4), lax.rem(s, 2)

    def tile_cols(tile):
        return pl.ds(pl.multiple_of(tile * HID_TILE, HID_TILE), HID_TILE)

    def begin(s):
        tile, block, slot = where_is(s)
        cols = tile_cols(tile)
        fetch(
            block, own1, got1,
            lambda src: pltpu.make_async_copy(
                src.at[:, cols], r.w1.at[slot], r.w_sems.at[slot, 0]
            ).start(),
        )
        fetch(
            block, own2, got2,
            lambda src: pltpu.make_async_copy(
                src.at[cols], r.w2.at[slot], r.w_sems.at[slot, 1]
            ).start(),
        )

    def out_copies(s):
        tile, block, slot = where_is(s)
        return [
            pltpu.make_async_copy(
                r.stage1.at[slot], targets[0].at[block, tile_cols(tile)], r.s_sems.at[slot, 0]
            ),
            pltpu.make_async_copy(
                r.stage2.at[slot], targets[1].at[block, tile_cols(tile)], r.s_sems.at[slot, 1]
            ),
        ]

    begin(0)

    def step(s):
        tile, block, slot = where_is(s)
        cols = tile_cols(tile)

        @pl.when(s + 1 < steps)
        def _():
            begin(s + 1)

        pltpu.make_async_copy(own1.at[:, cols], r.w1.at[slot], r.w_sems.at[slot, 0]).wait()
        pltpu.make_async_copy(own2.at[cols], r.w2.at[slot], r.w_sems.at[slot, 1]).wait()
        rows, grads = rows_ref[0:length], low[0:length]
        w1, w2 = r.w1[slot], r.w2[slot]
        preact = mm(rows, w1, NN) + hidden_bias(r, layer, block, tile)
        hidden_grad = mm(grads, w2, NT)
        half, decay = gelu_parts(preact)
        hidden = (preact * half).astype(BF16)
        pre_grad = (hidden_grad * (half + preact * (inv_root_tau * decay))).astype(BF16)
        if acc_out is not None:
            acc_out[0:length] += mm(hidden, w2, NN)
        r.stage2[slot] = mm(hidden, grads, TN).astype(BF16)
        row = pl.ds(pl.multiple_of(head + 8 * block, 8), 8)
        sums = jnp.sum(pre_grad.astype(F32), axis=0, keepdims=True)
        r.little[0, row, cols] += jnp.where(
            lax.broadcasted_iota(jnp.int32, (8, HID_TILE), 0) == b1_row, sums, 0.0
        )
        r.stage1[slot] = mm(pre_grad, rows, TN).astype(BF16)
        acc_back[0:length] += mm(pre_grad, w1, NT)
        for item in out_copies(s):
            item.start()

        @pl.when(lax.rem(s, 2) == 1)
        def _():
            for item in out_copies(s - 1) + out_copies(s):
                item.wait()

        after(s)

    loop(steps, step)


def attention_phase(r, layer, low, rows_ref, crops, acc_back, target, lane_at, after):
    length = crops[0].shape[0]
    own = r.attn.at[layer]
    got = r.got.at[3 * layer]
    qkv, ho = (r.qkv0, r.ho0) if layer == 0 else (r.qkv1, r.ho1)
    width = ho.shape[2]
    head_row = r.little.shape[1] - 32
    scale = HEAD_DIM**-0.5

    def begin(s):
        slot = lax.rem(s, 2)
        fetch(
            3 - s, own, got,
            lambda src: pltpu.make_async_copy(src, r.wa.at[slot], r.w_sems.at[slot, 0]).start(),
        )

    def out_copy(s):
        slot = lax.rem(s, 2)
        return pltpu.make_async_copy(r.stage_a.at[slot], target.at[3 - s], r.s_sems.at[slot, 0])

    begin(0)

    def step(s):
        slot, block = lax.rem(s, 2), 3 - s

        @pl.when(s < 3)
        def _():
            begin(s + 1)

        pltpu.make_async_copy(own, r.wa.at[slot], r.w_sems.at[slot, 0]).wait()
        grads = low[0:length]
        head_grads = mm(grads, r.wa[slot, 3 * width : 4 * width], NT).astype(BF16)
        r.stage_a[slot, 3 * width : 4 * width] = mm(ho[block], grads, TN).astype(BF16)
        for head in range(width // HEAD_DIM):
            q_at, k_at, v_at = [
                slice(i * width + head * HEAD_DIM, i * width + (head + 1) * HEAD_DIM)
                for i in range(3)
            ]
            q, k, v = qkv[block, :, q_at], qkv[block, :, k_at], qkv[block, :, v_at]
            gh = head_grads[:, q_at]
            scores, prob_grad = mm(k, q, NT), mm(v, gh, NT)
            scores = jnp.where(crops[0][...] == crops[1][...], scores, mask_fill)
            top = jnp.max(scores, axis=0, keepdims=True)
            weight = jnp.exp(scores - top)
            probs = weight * (1.0 / jnp.sum(weight, axis=0, keepdims=True))
            inner = jnp.sum(probs * prob_grad, axis=0, keepdims=True)
            score_grad = (probs * (prob_grad - inner)).astype(BF16)
            r.back[0:length, v_at] = mm(probs.astype(BF16), gh, NN).astype(BF16)
            r.back[0:length, k_at] = mm(score_grad, q, NN).astype(BF16)
            r.back[0:length, q_at] = (mm(score_grad, k, TN) * scale).astype(BF16)
        back = r.back[0:length]
        row = pl.ds(pl.multiple_of(head_row + 8 * block, 8), 8)
        first = lax.broadcasted_iota(jnp.int32, (8, width), 0) == 0
        for i, part in ((0, 0), (1, 2)):
            part_at = slice(part * width, (part + 1) * width)
            sums = jnp.sum(back[:, part_at].astype(F32), axis=0, keepdims=True)
            at = slice(lane_at + i * width, lane_at + (i + 1) * width)
            r.little[0, row, at] += jnp.where(first, sums, 0.0)
        r.stage_a[slot, 0 : 3 * width] = mm(back, rows_ref[0:length], TN).astype(BF16)
        acc_back[0:length] += mm(back, r.wa[slot, 0 : 3 * width], NN)
        out_copy(s).start()

        @pl.when(slot == 1)
        def _():
            out_copy(s - 1).wait()
            out_copy(s).wait()

        after(s)

    loop(4, step)


def layers_kernel(n_data, names, *refs):
    r = Names(names, refs)
    place = Place(n_data)
    n_bits = len(place.bits)
    length, features = r.image.shape
    picked = r.chosen.shape[0]
    width = r.ho0.shape[2]
    hidden = r.fc1.shape[2]
    part = slice(0, picked)

    gather = Gather(
        place,
        [ref.at[layer] for layer in range(2) for ref in (r.attn, r.fc1, r.fc2)],
        r.got,
        r.g_sends, r.g_recvs, r.near_sems, r.small, r.small_sends, r.small_recvs,
    )
    got_bits = [getattr(r, "got_bit" + str(i)) for i in range(n_bits)]
    sums = Sums(
        place, r.grads, r.sums,
        [r.own, r.far, r.got_own, r.got_far, r.got_y, r.total, got_bits]
        + [r.sends, r.recvs, r.loads, r.stores, r.turned],
    )
    little_sums = Butterfly(place, r.little, r.little_got, r.little_send, r.little_recv)

    def row_of(ref, number):
        return ref[...].astype(F32)[number : number + 1]

    def gain(layer, number):
        return row_of(r.norm_gain.at[layer], number)

    def normed(u, layer, number):
        xhat, _ = norm_parts(u)
        shift = row_of(r.norm_shift.at[layer], number)
        return (xhat * gain(layer, number) + shift).astype(BF16)

    shards = [
        (
            [
                pltpu.make_async_copy(
                    r.qkv_rows.at[layer], r.wa.at[layer, pl.ds(0, 3 * width)],
                    r.shard_sems.at[layer, 0],
                ),
                pltpu.make_async_copy(
                    r.out_weight.at[layer], r.wa.at[layer, pl.ds(3 * width, width)],
                    r.shard_sems.at[layer, 1],
                ),
            ],
            pltpu.make_async_copy(r.wa.at[layer], r.attn.at[layer], r.shard_sems.at[layer, 2]),
        )
        for layer in range(2)
    ]
    for loads, _ in shards:
        for item in loads:
            item.start()
    for layer in range(2):
        for number in range(2):
            lane = (2 * layer + number) * width
            r.small[0, :, lane : lane + width] = row_of(r.qv_bias.at[layer], number)
        lane = 4 * width + layer * hidden
        r.small[0, :, lane : lane + hidden] = row_of(r.fc1_bias, layer)
    for loads, store in shards:
        for item in loads:
            item.wait()
        store.start()
    greet([sums.core, sums.across] + sums.partners)
    gather.start([store for _, store in shards])

    route = r.route[pl.ds(place.tensor, 1)]
    ends, total = [], 0
    for crop in range(r.crops.shape[1]):
        total = total + r.crops[place.tensor, crop]
        ends.append(total)

    def crop_of(positions):
        found = jnp.zeros(positions.shape, F32)
        for end in ends:
            found = found + (positions >= end).astype(F32)
        return found

    r.crop_col_1[...] = crop_of(lax.broadcasted_iota(jnp.int32, (length, 1), 0))
    r.crop_row_1[...] = crop_of(lax.broadcasted_iota(jnp.int32, (1, length), 1))
    r.crop_row_0[...] = crop_of(route)
    spread = (lax.broadcasted_iota(jnp.int32, (length, picked), 0) == route).astype(F32)
    pick = jnp.transpose(spread)
    r.spread[...] = spread.astype(BF16)
    r.pick[...] = pick.astype(BF16)
    r.crop_col_0[...] = jnp.sum(pick * r.crop_row_1[...], axis=1, keepdims=True)
    r.chosen[...] = mm(r.pick[...], r.image[...], NN)
    router = r.router[...].astype(F32)
    r.rate[...] = 1.0 / (
        1.0 + jnp.exp(-jnp.sum(r.chosen[...] * router, axis=1, keepdims=True))
    )

    r.rows[part] = normed(r.chosen[...], 0, 0)
    r.acc_out[part] = r.chosen[...] + row_of(r.out_bias, 0)
    gather.small_turn()
    gather.near(0)

    def turns_before(s, steps, where, units):
        first = last = 0
        for step, k, k_end in steps:
            first = first + jnp.where(s == step, k, 0)
            last = last + jnp.where(s == step, k_end, 0)
        gather.turns(first, last)

        @pl.when(s == where)
        def _():
            for u in units:
                gather.far(u)

    def before_one(s):
        turns_before(s, ((0, 0, 1), (1, 1, 2), (2, 2, 4), (3, 4, 5)), 2, (0,))

    crops_0, crops_1 = (r.crop_col_0, r.crop_row_0), (r.crop_col_1, r.crop_row_1)
    attention_forward_phase(r, 0, r.rows, crops_0, r.acc_out, before_one)
    r.middle[...] = r.acc_out[part]
    r.rows[part] = normed(r.middle[...], 0, 1)
    r.acc_out[part] = r.middle[...] + row_of(r.fc2_bias, 0)
    gather.near(1)
    gather.near(2)

    def before_two(s):
        turns_before(s, ((0, 5, 6), (6, 6, 8), (9, 8, 9)), 6, (1, 2))

    ffn_forward_phase(r, 0, picked, r.rows, r.acc_out, before_two)
    r.branches[...] = r.acc_out[part] - r.chosen[...]

    r.routed[...] = r.image[...].astype(F32) + pick_rows(
        r.spread[...], r.rate[...] * r.branches[...]
    )
    r.rows[...] = normed(r.routed[...], 1, 0)
    r.acc_out[...] = r.routed[...] + row_of(r.out_bias, 1)
    gather.near(3)

    def before_three(s):
        turns_before(s, ((0, 9, 10), (1, 10, 11), (2, 11, 12), (3, 12, 13)), 2, (3,))

    attention_forward_phase(r, 1, r.rows, crops_1, r.acc_out, before_three)
    r.after_attn[...] = r.acc_out[...]
    gather.turns(13, 14)
    for u in (4, 5):
        gather.near(u)
        gather.far(u)
    r.little[0] = jnp.zeros_like(r.little[0])

    def put(row, value):
        r.little[0, row : row + 1] = value

    def back_through(u, layer, number):
        back, gain_part, shift_part = norm_back(
            r.acc_back[0 : u.shape[0]], u[...], gain(layer, number)
        )
        put(1 + 2 * layer + number, gain_part)
        put(5 + 2 * layer + number, shift_part)
        return back

    def lower(g, at, bias_row):
        r.low[at] = g.astype(BF16)
        put(bias_row, jnp.sum(r.low[at].astype(F32), axis=0, keepdims=True))
        r.acc_back[at] = jnp.zeros((at.stop, features), F32)

    everything = slice(0, length)

    def turns_at(s, steps):
        due, t = False, 0
        for step, number in steps:
            due, t = jnp.logical_or(due, s == step), t + jnp.where(s == step, number, 0)

        @pl.when(due)
        def _():
            sums.turn(t)

    r.rows[...] = normed(r.after_attn[...], 1, 1)
    lower(r.cotangent[...], everything, 12)
    r.acc_out[...] = r.after_attn[...] + row_of(r.fc2_bias, 1)

    def after_ffn_two(s):
        turns_at(s, ((1, 0), (2, 1), (5, 2), (7, 3), (9, 4)))

    ffn_phase(
        r, 1, length, r.low, r.rows, r.acc_out, r.acc_back, (r.grads.at[0], r.grads.at[1]), 2,
        after_ffn_two,
    )
    r.images_out[...] = r.acc_out[...].astype(BF16)
    grad = r.input_grad
    grad[...] = r.cotangent[...].astype(F32) + back_through(r.after_attn, 1, 1)

    r.rows[...] = normed(r.routed[...], 1, 0)
    lower(grad[...], everything, 10)
    attention_phase(
        r, 1, r.low, r.rows, crops_1, r.acc_back, r.grads.at[2], 2 * width,
        lambda s: sums.turn(5 + s),
    )
    grad[...] += back_through(r.routed, 1, 0)

    g_chosen = pick_rows(r.pick[...], grad[...])
    rate = r.rate[...]
    g_logit = jnp.sum(g_chosen * r.branches[...], axis=1, keepdims=True) * rate * (1.0 - rate)
    put(0, jnp.sum(r.chosen[...] * g_logit, axis=0, keepdims=True))
    r.g_branch[...] = rate * g_chosen

    r.rows[part] = normed(r.middle[...], 0, 1)
    lower(r.g_branch[...], part, 11)

    def after_ffn_one(s):
        turns_at(s, ((1, 9), (3, 10), (6, 11), (9, 12), (11, 13)))

    ffn_phase(
        r, 0, picked, r.low, r.rows, None, r.acc_back, (r.grads.at[3], r.grads.at[4]), 1, after_ffn_one
    )
    g_middle = r.g_branch[...] + back_through(r.middle, 0, 1)
    r.acc_out[part] = g_middle

    r.rows[part] = normed(r.chosen[...], 0, 0)
    lower(g_middle, part, 9)

    def after_attention_one(s):
        sums.turn(14 + s)

    attention_phase(
        r, 0, r.low, r.rows, crops_0, r.acc_back, r.grads.at[5], 0, after_attention_one
    )
    own_grad = g_logit * router + (r.acc_out[part] + back_through(r.chosen, 0, 0) - r.g_branch[...])
    little_sums.turn(0)
    grad[...] += pick_rows(r.spread[...], own_grad)

    first = 18
    last = sums.count + len(sums.stages) - 1

    def rest(i):
        t = first + i
        sums.turn(t)
        for number in range(len(little_sums.ways)):

            @pl.when(i == number)
            def _():
                little_sums.turn(number + 1)

    loop(last - first, rest)
    r.little_out[...] = r.little[len(little_sums.ways)]
    gather.finish()


def layers(arrays):
    n_data, group = lax.axis_size("dp"), lax.axis_size("tensor")
    n_bits = n_data.bit_length() - 1
    length, features = arrays["image"].shape
    picked = arrays["route"].shape[1]
    width = arrays["qv_bias"].shape[2]
    rows = 4 * width
    hidden = arrays["fc1"].shape[2]
    chunk_rows = rows // 3
    n_line = 18
    n_ways = n_bits + 2
    little_rows = 16 + 8 * group
    vmem = pl.BlockSpec(memory_space=pltpu.VMEM)
    places = {name: any_spec for name in ("qkv_rows", "out_weight", "fc1", "fc2")}
    places["crops"] = pl.BlockSpec(memory_space=pltpu.SMEM)
    units = 6
    outs = {
        "images_out": ((length, features), BF16, vmem),
        "input_grad": ((length, features), F32, vmem),
        "little_out": ((little_rows, features), F32, vmem),
    }
    outs["attn"] = ((2, rows, features), BF16, any_spec)
    outs["sums"] = ((units, rows, features), BF16, any_spec)
    outs["grads"] = ((units, group, rows, features), BF16, any_spec)
    outs["got"] = ((units, group - 1, rows, features), BF16, any_spec)
    dma, mem = pltpu.SemaphoreType.DMA, pltpu.VMEM
    scratch = {
        "g_sends": dma((2 * units, len(KINDS))),
        "g_recvs": dma((2 * units, len(KINDS))),
        "near_sems": dma((2, units)),
        "small": mem((group, 1, 4 * width + 2 * hidden), F32),
        "shard_sems": dma((2, 3)),
        "small_sends": dma((3,)),
        "small_recvs": dma((3,)),
        "crop_col_0": mem((picked, 1), F32),
        "crop_row_0": mem((1, picked), F32),
        "crop_col_1": mem((length, 1), F32),
        "crop_row_1": mem((1, length), F32),
        "spread": mem((length, picked), BF16),
        "pick": mem((picked, length), BF16),
        "chosen": mem((picked, features), F32),
        "rate": mem((picked, 1), F32),
        "middle": mem((picked, features), F32),
        "branches": mem((picked, features), F32),
        "routed": mem((length, features), F32),
        "after_attn": mem((length, features), F32),
        "qkv0": mem((group, picked, 3 * width), BF16),
        "ho0": mem((group, picked, width), BF16),
        "qkv1": mem((group, length, 3 * width), BF16),
        "ho1": mem((group, length, width), BF16),
        "rows": mem((length, features), BF16),
        "low": mem((length, features), BF16),
        "acc_out": mem((length, features), F32),
        "acc_back": mem((length, features), F32),
        "g_branch": mem((picked, features), F32),
        "w1": mem((2, features, HID_TILE), BF16),
        "w2": mem((2, HID_TILE, features), BF16),
        "stage1": mem((2, HID_TILE, features), BF16),
        "stage2": mem((2, HID_TILE, features), BF16),
        "wa": mem((2, rows, features), BF16),
        "stage_a": mem((2, rows, features), BF16),
        "back": mem((length, 3 * width), BF16),
        "w_sems": dma((2, 2)),
        "s_sems": dma((2, 2)),
        "own": mem((SLOTS, chunk_rows, features), BF16),
        "far": mem((SLOTS, chunk_rows, features), BF16),
        "got_own": mem((SLOTS, chunk_rows, features), BF16),
        "got_far": mem((SLOTS, chunk_rows, features), BF16),
        "got_y": mem((SLOTS, chunk_rows, features), BF16),
        "total": mem((SLOTS, chunk_rows, features), BF16),
        "turned": mem((2, features, chunk_rows), BF16),
        "sends": dma((3 + 2 * n_bits, n_line)),
        "recvs": dma((3 + 2 * n_bits, n_line)),
        "loads": dma((2, n_line)),
        "stores": dma((n_line,)),
        "little": mem((n_ways + 1, little_rows, features), F32),
        "little_got": mem((n_ways, little_rows, features), F32),
        "little_send": dma((n_ways,)),
        "little_recv": dma((n_ways,)),
    }
    for i, piece in enumerate(piece_shapes(n_bits, chunk_rows, features)):
        scratch["got_bit" + str(i)] = mem((SLOTS,) + piece, BF16)
    names = list(arrays) + list(outs) + list(scratch)
    flops = 2 * features * (8 * length + 7 * picked) * 4 * hidden
    result = pl.pallas_call(
        functools.partial(layers_kernel, n_data, names),
        out_shape=[jax.ShapeDtypeStruct(shape, dtype) for shape, dtype, _ in outs.values()],
        in_specs=[places.get(name, vmem) for name in arrays],
        out_specs=[item[2] for item in outs.values()],
        scratch_shapes=list(scratch.values()),
        compiler_params=pltpu.CompilerParams(
            collective_id=1, has_side_effects=True, vmem_limit_bytes=62 * 1024 * 1024
        ),
        name="layers",
        cost_estimate=pl.CostEstimate(
            flops=flops, transcendentals=length * hidden * 8, bytes_accessed=200 * 1024 * 1024
        ),
    )(*arrays.values())
    return dict(zip(outs, result))


def results_kernel(names, *refs):
    r = Names(names, refs)
    held, wide = r.held, r.wide
    count, rows = held.shape[:2]
    width = r.out_weight.shape[1]
    loads = [
        pltpu.make_async_copy(r.sums.at[u], held.at[u], r.in_sems.at[u]) for u in range(count)
    ]
    others = [
        pltpu.make_async_copy(r.images_in, r.held_images, r.other_sems.at[0]),
        pltpu.make_async_copy(r.grad_in, r.held_grad, r.other_sems.at[1]),
    ]
    for item in loads[:2] + others + loads[2:]:
        item.start()
    little = r.little
    r.router[...] = little[0:1]
    for layer in range(2):
        for number in range(2):
            at = (2 * layer + number) * width
            row = 2 * layer + number
            r.gain[layer, number : number + 1] = little[1 + row : 2 + row]
            r.shift[layer, number : number + 1] = little[5 + row : 6 + row]
            r.qv_bias[layer, number : number + 1] = little[16:17, at : at + width]
    r.out_bias[...] = little[9:11]
    r.fc2_bias[...] = little[11:13]
    r.fc1_bias[...] = little[17:19]
    for item in others:
        item.wait()
    stores = [
        pltpu.make_async_copy(r.held_images, r.images_out.at[0], r.other_sems.at[2]),
        pltpu.make_async_copy(r.held_grad, r.input_grad.at[0], r.other_sems.at[3]),
    ]
    for item in stores:
        item.start()
    for u in range(count):
        layer, kind = 1 - u // 3, u % 3
        loads[u].wait()
        wide[u] = held[u].astype(F32)
        if kind == 2:
            stores += [
                pltpu.make_async_copy(
                    wide.at[u, pl.ds(0, rows - width)], r.qkv.at[layer], r.out_sems.at[u, 0]
                ),
                pltpu.make_async_copy(
                    wide.at[u, pl.ds(rows - width, width)], r.out_weight.at[layer],
                    r.out_sems.at[u, 1],
                ),
            ]
            stores[-2].start()
        else:
            target = (r.fc1, r.fc2)[kind].at[layer]
            stores.append(pltpu.make_async_copy(wide.at[u], target, r.out_sems.at[u, 0]))
        stores[-1].start()
    for item in stores:
        item.wait()


def results(res, width):
    little, sums = res["little_out"], res["sums"]
    count, rows, features = sums.shape
    length = res["images_out"].shape[0]
    vmem = pl.BlockSpec(memory_space=pltpu.VMEM)
    outs = {
        "images_out": ((1, length, features), BF16, any_spec),
        "input_grad": ((1, length, features), F32, any_spec),
        "router": ((1, features), F32, vmem),
        "gain": ((2, 2, features), F32, vmem),
        "shift": ((2, 2, features), F32, vmem),
        "qkv": ((2, rows - width, features), F32, any_spec),
        "qv_bias": ((2, 2, width), F32, vmem),
        "out_weight": ((2, width, features), F32, any_spec),
        "out_bias": ((2, features), F32, vmem),
        "fc1": ((2, rows, features), F32, any_spec),
        "fc1_bias": ((2, features), F32, vmem),
        "fc2": ((2, rows, features), F32, any_spec),
        "fc2_bias": ((2, features), F32, vmem),
    }
    dma = pltpu.SemaphoreType.DMA
    scratch = {
        "held": pltpu.VMEM((count, rows, features), BF16),
        "wide": pltpu.VMEM((count, rows, features), F32),
        "in_sems": dma((count,)),
        "out_sems": dma((count, 2)),
        "held_images": pltpu.VMEM((length, features), BF16),
        "held_grad": pltpu.VMEM((length, features), F32),
        "other_sems": dma((4,)),
    }
    inputs = ["sums", "little", "images_in", "grad_in"]
    hbm = pl.BlockSpec(memory_space=pltpu.HBM)
    return pl.pallas_call(
        functools.partial(results_kernel, inputs + list(outs) + list(scratch)),
        out_shape=[jax.ShapeDtypeStruct(shape, dtype) for shape, dtype, _ in outs.values()],
        in_specs=[hbm, vmem, hbm, hbm],
        out_specs=[item[2] for item in outs.values()],
        scratch_shapes=list(scratch.values()),
        compiler_params=pltpu.CompilerParams(vmem_limit_bytes=62 * 1024 * 1024),
        name="results",
    )(sums, little, res["images_out"], res["input_grad"])


def body(
    images_in,
    crop_lengths,
    route_index,
    router_weight,
    norm_gain,
    norm_shift,
    qkv_weight,
    qv_bias,
    out_weight,
    out_bias,
    fc1_weight,
    fc1_bias,
    fc2_weight,
    fc2_bias,
    out_cotangent,
):
    features = images_in.shape[2]
    width = qkv_weight.shape[-1]

    qkv_rows = jnp.swapaxes(qkv_weight, 2, 3).reshape(2, 3 * width, features)
    res = layers(
        {
            "image": images_in[0], "cotangent": out_cotangent[0], "route": route_index,
            "crops": crop_lengths, "router": router_weight[None, :], "norm_gain": norm_gain,
            "norm_shift": norm_shift, "qv_bias": qv_bias, "fc1_bias": fc1_bias,
            "out_bias": out_bias, "fc2_bias": fc2_bias,
            "qkv_rows": qkv_rows, "out_weight": out_weight, "fc1": fc1_weight, "fc2": fc2_weight,
        }
    )
    out = list(results(res, width))
    out[2] = out[2].reshape(features)
    out[5] = jnp.swapaxes(out[5].reshape(2, 3, width, features), 2, 3)
    return tuple(out)


def solution(mesh):
    in_specs = (
        P(("dp", "tensor"), None, None),
        P("dp", None),
        P("dp", None),
        P(),
        P(),
        P(),
        P(None, None, None, "tensor"),
        P(None, None, "tensor"),
        P(None, "tensor", None),
        P(),
        P(None, None, "tensor"),
        P(None, "tensor"),
        P(None, "tensor", None),
        P(),
        P(("dp", "tensor"), None, None),
    )
    out_specs = (
        P(("dp", "tensor"), None, None),
        P(("dp", "tensor"), None, None),
        P(),
        P(),
        P(),
        P(None, None, None, "tensor"),
        P(None, None, "tensor"),
        P(None, "tensor", None),
        P(),
        P(None, None, "tensor"),
        P(None, "tensor"),
        P(None, "tensor", None),
        P(),
    )
    return jax.shard_map(body, mesh=mesh, in_specs=in_specs, out_specs=out_specs, check_vma=False)
```

profile of v0, /device:TPU:0, one launch (start us, length us, event | category | flops | bytes accessed | tf_op | source)
XLA Modules:
  0.0 312.6 jit_solution(891078376679988851)
XLA Ops:
  0.6 1.3 broadcast_in_dim.3.refs_4_
  1.9 298.4 %layers.1 = (bf16[544,768]{1,0:T(8,128)(2,1)}, f32[544,768]{1,0:T(8,128)}, f32[48,768]{1,0:T(8,128)}, bf16[2,768,768]{2,1,0:T(8,128)(2,1)}, bf16[6,768,768]{2,1,...) custom-call(bf16[544,768]{1,0:T(8,128)(2,1)} %bitcast.10, bf16[544,768]{1,0:T(8,128)(2,1)} %bitcast.11, ...), custom_call_target="tpu_custom_call" | custom-call | flops 29519511552 | bytes 209715200 | tf_op jit(solution)/shard_map/layers/pallas_call | solution.py:1053
  300.3 11.0 %results.1 = (bf16[1,544,768]{2,1,0:T(8,128)(2,1)}, f32[1,544,768]{2,1,0:T(8,128)}, f32[1,768]{1,0:T(1,128)}, f32[2,2,768]{2,1,0:T(2,128)}, f32[2,2,768]{2,1,0:T...) custom-call(bf16[6,768,768]{2,1,0:T(8,128)(2,1)} %get-tuple-element., ...), custom_call_target="tpu_custom_call" | custom-call | tf_op jit(solution)/shard_map/results/pallas_call | solution.py:1159
  311.3 1.3 reduce
where the time goes:
time: 313 us
  Pallas kernels  309 us (99%)
    pallas_call x1, Pallas kernels, layers(): pl.pallas_call(functools.partial(layers_kernel, n_data, names), out_shape...  298 us
    pallas_call x1, Pallas kernels, results(): pl.pallas_call(functools.partial(results_kernel, inputs + list(outs) + li...  11 us

commit v1 on v0

--- a/solution.py
+++ b/solution.py
@@ -811,7 +811,7 @@
     r.pick[...] = pick.astype(BF16)
     r.crop_col_0[...] = jnp.sum(pick * r.crop_row_1[...], axis=1, keepdims=True)
     r.chosen[...] = mm(r.pick[...], r.image[...], NN)
-    router = r.router[...].astype(F32)
+    router = r.router[...].astype(F32).reshape(1, features)
     r.rate[...] = 1.0 / (
         1.0 + jnp.exp(-jnp.sum(r.chosen[...] * router, axis=1, keepdims=True))
     )
@@ -845,7 +845,7 @@
     gather.near(2)
 
     def before_two(s):
-        turns_before(s, ((0, 5, 6), (6, 6, 8), (9, 8, 9)), 6, (1, 2))
+        turns_before(s, ((0, 5, 6), (3, 6, 7), (6, 7, 8), (9, 8, 9)), 6, (1, 2))
 
     ffn_forward_phase(r, 0, picked, r.rows, r.acc_out, before_two)
     r.branches[...] = r.acc_out[part] - r.chosen[...]
@@ -906,8 +906,10 @@
         r, 1, length, r.low, r.rows, r.acc_out, r.acc_back, (r.grads.at[0], r.grads.at[1]), 2,
         after_ffn_two,
     )
-    r.images_out[...] = r.acc_out[...].astype(BF16)
-    grad = r.input_grad
+    r.images[...] = r.acc_out[...].astype(BF16)
+    images_done = pltpu.make_async_copy(r.images, r.images_out, r.done_sems.at[0])
+    images_done.start()
+    grad = r.grad
     grad[...] = r.cotangent[...].astype(F32) + back_through(r.after_attn, 1, 1)
 
     r.rows[...] = normed(r.routed[...], 1, 0)
@@ -948,6 +950,8 @@
     own_grad = g_logit * router + (r.acc_out[part] + back_through(r.chosen, 0, 0) - r.g_branch[...])
     little_sums.turn(0)
     grad[...] += pick_rows(r.spread[...], own_grad)
+    grad_done = pltpu.make_async_copy(grad, r.input_grad, r.done_sems.at[1])
+    grad_done.start()
 
     first = 18
     last = sums.count + len(sums.stages) - 1
@@ -964,6 +968,8 @@
     loop(last - first, rest)
     r.little_out[...] = r.little[len(little_sums.ways)]
     gather.finish()
+    images_done.wait()
+    grad_done.wait()
 
 
 def layers(arrays):
@@ -983,8 +989,8 @@
     places["crops"] = pl.BlockSpec(memory_space=pltpu.SMEM)
     units = 6
     outs = {
-        "images_out": ((length, features), BF16, vmem),
-        "input_grad": ((length, features), F32, vmem),
+        "images_out": ((length, features), BF16, any_spec),
+        "input_grad": ((length, features), F32, any_spec),
         "little_out": ((little_rows, features), F32, vmem),
     }
     outs["attn"] = ((2, rows, features), BF16, any_spec)
@@ -997,6 +1003,9 @@
         "g_recvs": dma((2 * units, len(KINDS))),
         "near_sems": dma((2, units)),
         "small": mem((group, 1, 4 * width + 2 * hidden), F32),
+        "images": mem((length, features), BF16),
+        "grad": mem((length, features), F32),
+        "done_sems": dma((2,)),
         "shard_sems": dma((2, 3)),
         "small_sends": dma((3,)),
         "small_recvs": dma((3,)),
@@ -1082,7 +1091,7 @@
     for item in loads[:2] + others + loads[2:]:
         item.start()
     little = r.little
-    r.router[...] = little[0:1]
+    r.router[...] = little[0]
     for layer in range(2):
         for number in range(2):
             at = (2 * layer + number) * width
@@ -1132,7 +1141,7 @@
     outs = {
         "images_out": ((1, length, features), BF16, any_spec),
         "input_grad": ((1, length, features), F32, any_spec),
-        "router": ((1, features), F32, vmem),
+        "router": ((features,), F32, vmem),
         "gain": ((2, 2, features), F32, vmem),
         "shift": ((2, 2, features), F32, vmem),
         "qkv": ((2, rows - width, features), F32, any_spec),
@@ -1191,14 +1200,13 @@
     res = layers(
         {
             "image": images_in[0], "cotangent": out_cotangent[0], "route": route_index,
-            "crops": crop_lengths, "router": router_weight[None, :], "norm_gain": norm_gain,
+            "crops": crop_lengths, "router": router_weight, "norm_gain": norm_gain,
             "norm_shift": norm_shift, "qv_bias": qv_bias, "fc1_bias": fc1_bias,
             "out_bias": out_bias, "fc2_bias": fc2_bias,
             "qkv_rows": qkv_rows, "out_weight": out_weight, "fc1": fc1_weight, "fc2": fc2_weight,
         }
     )
     out = list(results(res, width))
-    out[2] = out[2].reshape(features)
     out[5] = jnp.swapaxes(out[5].reshape(2, 3, width, features), 2, 3)
     return tuple(out)
 

time: 313 us -> 308 us (0.984)
  no operation moved by 1% of the time
where the time goes in v1:
time: 308 us; the launch traced here: 307 us
  Pallas kernels  307 us (100%)
    pallas_call x1, Pallas kernels, layers(): pl.pallas_call(functools.partial(layers_kernel, n_data, names), out_shape...  296 us
    pallas_call x1, Pallas kernels, results(): pl.pallas_call(functools.partial(results_kernel, inputs + list(outs) + li...  11 us

profile of v1, /device:TPU:0, one launch (start us, length us, event | category | flops | bytes accessed | tf_op | source)
XLA Modules:
  0.0 307.5 jit_solution(202031000351160508)
XLA Ops:
  0.7 295.6 %layers.1 = (bf16[544,768]{1,0:T(8,128)(2,1)}, f32[544,768]{1,0:T(8,128)}, f32[48,768]{1,0:T(8,128)}, bf16[2,768,768]{2,1,0:T(8,128)(2,1)}, bf16[6,768,768]{2,1,...) custom-call(bf16[544,768]{1,0:T(8,128)(2,1)} %bitcast.10, bf16[544,768]{1,0:T(8,128)(2,1)} %bitcast.11, ...), custom_call_target="tpu_custom_call" | custom-call | flops 29519511552 | bytes 209715200 | tf_op jit(solution)/shard_map/layers/pallas_call | solution.py:1062
  296.3 11.0 %results.1 = (bf16[1,544,768]{2,1,0:T(8,128)(2,1)}, f32[1,544,768]{2,1,0:T(8,128)}, f32[768]{0:T(1024)}, f32[2,2,768]{2,1,0:T(2,128)}, f32[2,2,768]{2,1,0:T(2,12...) custom-call(bf16[6,768,768]{2,1,0:T(8,128)(2,1)} %get-tuple-element., ...), custom_call_target="tpu_custom_call" | custom-call | tf_op jit(solution)/shard_map/results/pallas_call | solution.py:1168

commit v2 on v1

--- a/solution.py
+++ b/solution.py
@@ -399,7 +399,7 @@
     def __init__(self, place, stages, got, sends, recvs):
         self.stages, self.got, self.sends, self.recvs = stages, got, sends, recvs
         self.n_bits = len(place.bits)
-        self.ways = [place.by_data(i) for i in range(self.n_bits)]
+        self.ways = [place.by_data(i) for i in reversed(range(self.n_bits))]
         self.ways += [place.by_tensor(1), place.by_tensor(2)]
         self.head = stages.shape[1] - 8 * 4
 

time: 308 us -> 307 us (level)
  no operation moved by 1% of the time
where the time goes in v2:
time: 307 us; the launch traced here: 306 us
  Pallas kernels  305 us (99%)
    pallas_call x1, Pallas kernels, layers(): pl.pallas_call(functools.partial(layers_kernel, n_data, names), out_shape...  294 us
    pallas_call x1, Pallas kernels, results(): pl.pallas_call(functools.partial(results_kernel, inputs + list(outs) + li...  11 us

profile of v2, /device:TPU:0, one launch (start us, length us, event | category | flops | bytes accessed | tf_op | source)
XLA Modules:
  0.0 306.2 jit_solution(7899129832008495102)
XLA Ops:
  0.7 294.4 %layers.1 = (bf16[544,768]{1,0:T(8,128)(2,1)}, f32[544,768]{1,0:T(8,128)}, f32[48,768]{1,0:T(8,128)}, bf16[2,768,768]{2,1,0:T(8,128)(2,1)}, bf16[6,768,768]{2,1,...) custom-call(bf16[544,768]{1,0:T(8,128)(2,1)} %bitcast.10, bf16[544,768]{1,0:T(8,128)(2,1)} %bitcast.11, ...), custom_call_target="tpu_custom_call" | custom-call | flops 29519511552 | bytes 209715200 | tf_op jit(solution)/shard_map/layers/pallas_call | solution.py:1062
  295.0 11.0 %results.1 = (bf16[1,544,768]{2,1,0:T(8,128)(2,1)}, f32[1,544,768]{2,1,0:T(8,128)}, f32[768]{0:T(1024)}, f32[2,2,768]{2,1,0:T(2,128)}, f32[2,2,768]{2,1,0:T(2,12...) custom-call(bf16[6,768,768]{2,1,0:T(8,128)(2,1)} %get-tuple-element., ...), custom_call_target="tpu_custom_call" | custom-call | tf_op jit(solution)/shard_map/results/pallas_call | solution.py:1168
